TPU v7x, 512 devices: a whole 4x8x8 slice. The times are simulated.
512 devices in a mesh: ctx: 32 (over x, z_hi, core), tp: 16 (over y, z_lo).
Axes of the slice: x: 4, y: 8, z: 8 (z_hi: 4, z_lo: 2; z = z_hi * 2 + z_lo), core: 2. Of those that a mesh axis runs over, the one named last changes fastest.
Arguments:
- queries: bfloat16 [8192, 2048], P('ctx', 'tp'), may hold values from -24 to 24
- key_heads: bfloat16 [8192, 4, 128], P('ctx'), may hold values from -6 to 6
- head_values: bfloat16 [8192, 4, 128], P('ctx'), may hold values from -6 to 6
- hidden: bfloat16 [8192, 4096], P('ctx'), may hold values from -0.59765625 to 0.59765625
- out_proj: bfloat16 [2048, 4096], P('tp'), may hold values from -0.125 to 0.125
- norm_gain: float32 [4096], replicated, may hold values from 0.25 to 1.75
- x_proj: bfloat16 [4096, 4096], P('ctx', 'tp'), may hold values from -0.046875 to 0.046875
- bc_proj: bfloat16 [4096, 4, 256], P('ctx'), may hold values from -0.09375 to 0.09375
- dt_proj: bfloat16 [4096, 64], P('ctx', 'tp'), may hold values from -0.09375 to 0.09375
- dt_bias: float32 [64], P('tp'), may hold values from -12 to 0
- decay_log: float32 [64], P('tp'), may hold values from -10 to 3
- skip_gain: float32 [64], P('tp'), may hold values from 0.5 to 1.5
Outputs:
- residual_out: bfloat16 [8192, 4096], P('ctx', 'tp')
- mamba_out: bfloat16 [8192, 4096], P('ctx', 'tp')
All inputs are finite; a program needn't handle non-finite values.
Results may differ from a plain program's by a relative error of at most 0.034.
Values may be sent and summed in bfloat16 or wider, within the bound.
No kernel may reach another device: no remote copies, remote signals or barrier semaphores. Data moves between devices by JAX's collectives and lax.ppermute only.
A program may use at most 64 MiB of HBM per device.

v0:
```python
import math
import jax
import jax.numpy as jnp
from jax import lax
from jax.sharding import PartitionSpec as P


def prefix(value, axis, join, neutral, backward):
    count, mine = (lax.axis_size(axis), lax.axis_index(axis))
    pieces = jax.tree.map(lambda part: lax.all_gather(part, axis), value)
    if backward:
        pieces = jax.tree.map(lambda part: part[::-1], pieces)
        mine = count - 1 - mine
    so_far = jax.tree.map(
        lambda part, zero: jnp.full_like(part, 0) + jnp.asarray(zero, part.dtype), value, neutral
    )

    def lap(position, so_far):
        longer = join(so_far, jax.tree.map(lambda part: part[position], pieces))
        return jax.tree.map(lambda new, old: jnp.where(position < mine, new, old), longer, so_far)

    return lax.fori_loop(0, count - 1, lap, so_far)


def chain(earlier, later):
    return (earlier[0] * later[0], later[0][..., None, None] * earlier[1] + later[1])


def block_positions(rows, tok_dev, n_ctx):
    half = tok_dev // 2
    device = rows // tok_dev
    within = rows % tok_dev
    block = jnp.where(within < half, device, 2 * n_ctx - 1 - device)
    return block * half + within % half


def split_product(form, wide, narrow):
    upper = wide.astype(jnp.bfloat16)
    lower = (wide - upper.astype(jnp.float32)).astype(jnp.bfloat16)
    first_term = jnp.einsum(form, upper, narrow, preferred_element_type=jnp.float32)
    return first_term + jnp.einsum(form, lower, narrow, preferred_element_type=jnp.float32)


def body(
    queries,
    key_heads,
    head_values,
    hidden,
    out_proj,
    norm_gain,
    x_proj,
    bc_proj,
    dt_proj,
    dt_bias,
    decay_log,
    skip_gain,
):
    tok_dev = queries.shape[0]
    half = tok_dev // 2
    n_ctx = lax.axis_size("ctx")
    n_tp = lax.axis_size("tp")
    ctx_index = lax.axis_index("ctx")
    tp_index = lax.axis_index("tp")
    head_dim = key_heads.shape[2]
    kv_total = key_heads.shape[1]
    q_local = queries.shape[1] // head_dim
    group = q_local * n_tp // kv_total
    kv_local = max(1, q_local // group)
    per_kv = q_local // kv_local
    kv_start = tp_index * q_local // group
    keys_mine = lax.dynamic_slice_in_dim(key_heads, kv_start, kv_local, 1)
    values_mine = lax.dynamic_slice_in_dim(head_values, kv_start, kv_local, 1)
    query_pos = block_positions(
        ctx_index * tok_dev + jnp.arange(tok_dev, dtype=jnp.int32), tok_dev, n_ctx
    )
    shaped_q = queries.reshape(tok_dev, kv_local, per_kv, head_dim)
    root_dim = math.sqrt(head_dim)
    start_max = jnp.full((kv_local, per_kv, tok_dev), -1e30, jnp.float32)
    run_max = start_max
    key_piece = lax.all_gather(keys_mine, "ctx", axis=0, tiled=True)
    value_piece = lax.all_gather(values_mine, "ctx", axis=0, tiled=True)
    count = key_piece.shape[0]
    key_pos = block_positions(jnp.arange(count, dtype=jnp.int32), tok_dev, n_ctx)
    scores = (
        jnp.einsum("qgjd,kgd->gjqk", shaped_q, key_piece, preferred_element_type=jnp.float32)
        / root_dim
    )
    allowed = key_pos[None, :] <= query_pos[:, None]
    piece_max = jnp.max(jnp.where(allowed, scores, -1e30), axis=-1)
    new_max = jnp.maximum(run_max, piece_max)
    weights = jnp.where(allowed, jnp.exp(scores - new_max[..., None]), 0.0)
    run_sum = jnp.sum(weights, axis=-1)
    update = jnp.einsum(
        "gjqk,kgd->gjqd",
        weights.astype(jnp.bfloat16),
        value_piece,
        preferred_element_type=jnp.float32,
    )
    accum = update
    run_max, run_sum, accum = (new_max, run_sum, accum)
    attended = (
        jnp.transpose(accum / run_sum[..., None], (2, 0, 1, 3))
        .reshape(tok_dev, q_local * head_dim)
        .astype(jnp.bfloat16)
    )
    head_part = jnp.dot(attended, out_proj, preferred_element_type=jnp.float32)
    slice_width = hidden.shape[1] // n_tp
    attention_sum = lax.psum(head_part.astype(jnp.bfloat16), "tp").astype(jnp.float32)
    residual = (hidden.astype(jnp.float32) + attention_sum).astype(jnp.bfloat16)
    residual_out = lax.dynamic_slice_in_dim(residual, tp_index * slice_width, slice_width, 1)
    as_float = residual.astype(jnp.float32)
    mean_square = jnp.mean(as_float * as_float, axis=-1, keepdims=True)
    normed = (as_float * lax.rsqrt(mean_square + 1e-05) * norm_gain).astype(jnp.bfloat16)
    m_local = skip_gain.shape[0]
    state_size = bc_proj.shape[2] // 2
    groups_all = bc_proj.shape[1]
    per_group = m_local * n_tp // groups_all
    g_local = max(1, m_local // per_group)
    heads_each = m_local // g_local
    g_start = tp_index * m_local // per_group
    head_width = x_proj.shape[1] // m_local
    bc_mine = lax.dynamic_slice_in_dim(bc_proj, g_start, g_local, 1).reshape(
        bc_proj.shape[0], g_local * 2 * state_size
    )
    sum_x = jnp.dot(
        normed,
        lax.all_gather(x_proj, "ctx", axis=0, tiled=True),
        preferred_element_type=jnp.float32,
    )
    sum_bc = jnp.dot(
        normed,
        lax.all_gather(bc_mine, "ctx", axis=0, tiled=True),
        preferred_element_type=jnp.float32,
    )
    sum_dt = jnp.dot(
        normed,
        lax.all_gather(dt_proj, "ctx", axis=0, tiled=True),
        preferred_element_type=jnp.float32,
    )
    inputs_low = sum_x.astype(jnp.bfloat16).reshape(2, half, g_local, heads_each, head_width)
    inputs = inputs_low.astype(jnp.float32)
    bc_round = sum_bc.astype(jnp.bfloat16).reshape(2, half, g_local, 2 * state_size)
    b_low = bc_round[..., :state_size]
    c_low = bc_round[..., state_size:]
    steps = jax.nn.softplus(sum_dt + dt_bias).reshape(2, half, g_local, heads_each)
    rates = -jnp.exp(decay_log).reshape(g_local, heads_each)
    cumul = jnp.transpose(jnp.cumsum(steps * rates, axis=1), (0, 2, 3, 1))
    step_rows = jnp.transpose(steps, (0, 2, 3, 1))
    gram = jnp.einsum("ckgn,csgn->cgks", c_low, b_low, preferred_element_type=jnp.float32)
    places = jnp.arange(half, dtype=jnp.int32)
    causal = places[None, :] <= places[:, None]
    gaps = cumul[..., :, None] - cumul[..., None, :]
    decay = jnp.where(causal, jnp.exp(jnp.where(causal, gaps, 0.0)), 0.0)
    mixing = gram[:, :, None] * decay * step_rows[..., None, :]
    inner = split_product("cgjks,csgjp->ckgjp", mixing, inputs_low)
    last = cumul[..., -1]
    tail = jnp.exp(last[..., None] - cumul) * step_rows
    weighted = jnp.transpose(tail, (0, 3, 1, 2))[..., None] * inputs
    block_state = split_product("csgjp,csgn->cgjpn", weighted, b_low)
    block_decay = jnp.exp(last)
    first = (block_decay[0], block_state[0])
    second = (block_decay[1], block_state[1])
    unit = (jnp.ones_like(first[0]), jnp.zeros_like(first[1]))
    before = prefix(first, "ctx", chain, unit, False)
    last_device = ctx_index == n_ctx - 1
    through = chain(before, first)
    joined = chain(through, second)
    sent = (
        jnp.where(last_device, joined[0], second[0]),
        jnp.where(last_device, joined[1], second[1]),
    )
    after = prefix(sent, "ctx", chain, unit, True)
    second_in = jnp.where(last_device, through[1], after[1])
    entering = jnp.stack([before[1], second_in])
    carried = jnp.transpose(jnp.exp(cumul), (0, 3, 1, 2))[..., None] * split_product(
        "cgjpn,ckgn->ckgjp", entering, c_low
    )
    output = inner + carried + skip_gain.reshape(g_local, heads_each)[:, :, None] * inputs
    mamba_out = output.reshape(tok_dev, m_local * head_width).astype(jnp.bfloat16)
    return (residual_out, mamba_out)


def solution(mesh):
    placed = (
        P("ctx", "tp"),
        P("ctx", None, None),
        P("ctx", None, None),
        P("ctx", None),
        P("tp", None),
        P(),
        P("ctx", "tp"),
        P("ctx", None, None),
        P("ctx", "tp"),
        P("tp"),
        P("tp"),
        P("tp"),
    )
    return jax.shard_map(
        body,
        mesh=mesh,
        in_specs=placed,
        out_specs=(P("ctx", "tp"), P("ctx", "tp")),
        check_vma=False,
    )
```

profile of v0, /device:TPU:1, one launch (start us, length us, event | category | flops | bytes accessed | tf_op | source)
XLA Modules:
  0.0 671.6 jit_solution(12906673132283992635)
XLA Ops:
  7.2 1.2 constant_dynamic-slice_fusion.4
  9.1 1.1 constant_dynamic-slice_fusion.3
  11.0 66.9 %all-gather.13.cloned.1.call-done = bf16[8192,1,128]{2,0,1:T(8,128)(2,1)} async-done(((bf16[256,1,128]{2,0,1:T(8,128)(2,1)}), bf16[8192,1,128]{2,0,1:T(8,128)(2,1)}) %all-gather.13.cloned.1.call-update) | async-done | bytes 2097168 | tf_op jit(solution)/shard_map/all_gather | solution.py:80
  77.9 5.7 fusion.4
  83.6 3.3 copy-done.1
  86.9 3.7 fusion.5
  90.7 48.6 %all-gather.15.cloned.1.call-done = bf16[8192,1,128]{2,0,1:T(8,128)(2,1)} async-done(((bf16[256,1,128]{2,0,1:T(8,128)(2,1)}), bf16[8192,1,128]{2,0,1:T(8,128)(2,1)}) %all-gather.15.cloned.1.call-update) | async-done | bytes 2097168 | tf_op jit(solution)/shard_map/all_gather | solution.py:81
  139.3 8.7 %convolution_convert_fusion = bf16[256,4096]{1,0:T(8,128)(2,1)} fusion(bf16[128,4096]{1,0:T(8,128)(2,1)S(1)} %copy-done, bf16[8192,1,128]{2,0,1:T(8,128)(2,1)} %all-gather.15.cloned.1.call-done, f32[1,1,256,8192]{2,3,1,0:T(8,128)} %copy-done.1, f32[256]{0:T(256)S(1)} %broadcast_maximum_fusion, s32[256]{0:T(256)S(1)} %fusion.88, s32[8192]{0:T(1024)S(1)} %fusion.83, ...), kind=kOutput, calls=%fused_computation.18 | convolution fusion | flops 814809088 | bytes 13667328 | tf_op jit(solution)/shard_map/dot_general | solution.py:106
  149.5 43.0 %all_gather.37 = bf16[4096,4]{0,1:T(4,128)(2,1)S(1)} all-gather(bf16[128,4]{0,1:T(4,128)(2,1)S(1)} %copy-done.14), channel_id=1, replica_groups=mesh['ctx'=32,'tp'=16] {'ctx'}, dimensions={0}, use_global_device_ids=true | all-gather | bytes 33792 | tf_op jit(solution)/shard_map/all_gather | solution.py:137
  192.5 94.5 %all-reduce.2.cloned.1.call-done = bf16[256,4096]{1,0:T(8,128)(2,1)} async-done(((bf16[256,4096]{1,0:T(8,128)(2,1)}), bf16[256,4096]{1,0:T(8,128)(2,1)}) %all-reduce.2.cloned.1.call-update) | async-done | bytes 2097168 | tf_op jit(solution)/shard_map/psum | solution.py:108
  287.0 3.2 fusion.7
  290.2 68.7 %all-gather.17.cloned.1.call-done = bf16[4096,256]{1,0:T(8,128)(2,1)} async-done(((bf16[128,256]{1,0:T(8,128)(2,1)}), bf16[4096,256]{1,0:T(8,128)(2,1)}) %all-gather.17.cloned.1.call-update) | async-done | bytes 2097168 | tf_op jit(solution)/shard_map/all_gather | solution.py:127
  358.9 2.4 convolution_convert_fusion.1
  362.1 1.1 copy.90
  365.1 55.0 %all-gather.19.cloned.1.call-done = bf16[4096,1,256]{2,0,1:T(8,128)(2,1)} async-done(((bf16[128,1,256]{2,0,1:T(8,128)(2,1)}), bf16[4096,1,256]{2,0,1:T(8,128)(2,1)}) %all-gather.19.cloned.1.call-update) | async-done | bytes 2097168 | tf_op jit(solution)/shard_map/all_gather | solution.py:132
  420.1 2.4 fusion.24
  423.1 1.1 convolution_add_fusion.1
  425.6 43.8 %all-gather.1 = f32[32,1,4,1]{2,3,1,0:T(1,128)} all-gather(f32[1,1,4,1]{2,3,1,0:T(1,128)S(1)} %get-tuple-element.328), channel_id=3, replica_groups=mesh['ctx'=32,'tp'=16] {'ctx'}, dimensions={0}, use_global_device_ids=true | all-gather | bytes 528 | tf_op jit(solution)/shard_map/all_gather | solution.py:10
  469.4 19.7 %all-gather.21.cloned.1.call-done = f32[32,4,64,128]{3,2,1,0:T(8,128)} async-done(((f32[1,4,64,128]{3,2,1,0:T(8,128)}), f32[32,4,64,128]{3,2,1,0:T(8,128)}) %all-gather.21.cloned.1.call-update) | async-done | bytes 4194320 | tf_op jit(solution)/shard_map/all_gather | solution.py:10
  489.1 70.9 %while.30 = (s32[]{:T(128)}, f32[1,4]{1,0:T(1,128)S(1)}, f32[1,4,64,128]{3,2,1,0:T(8,128)S(1)}, s32[]{:T(128)}, f32[32,1,4]{2,1,0:T(1,128)}, /*index=5*/f32[32,1,4,64,128]{4,3,2,1,0:T(8,128)}, s32[]{:T(128)}, s32[]{:T(128)}) while((s32[]{:T(128)}, f32[1,4]{1,0:T(1,128)S(1)}, f32[1,4,64,128]{3,2,1,0:T(8,128)S(1)}, s32[]{:T(128)}, ...), condition=%wide.region_6.7_spmd.clone, body=%wide.region_5.6_spmd.clone.sunk | while | flops 131088 | bytes 393431 | solution.py:22
  560.0 1.3 add_select_fusion
  561.4 2.0 reshape.405
  564.3 2.0 copy.102
  567.0 1.0 fusion.65
  568.0 1.3 fusion.50
  570.0 42.2 %all-gather.5 = f32[32,1,4]{2,1,0:T(1,128)S(1)} all-gather(f32[1,1,4]{2,1,0:T(1,128)S(1)} %fusion.91), channel_id=5, replica_groups=mesh['ctx'=32,'tp'=16] {'ctx'}, dimensions={0}, use_global_device_ids=true | all-gather | bytes 528 | tf_op jit(solution)/shard_map/all_gather | solution.py:10
  612.5 13.4 %all-gather.23.cloned.1.call-done = f32[32,4,64,128]{3,2,1,0:T(8,128)} async-done(((f32[1,4,64,128]{3,2,1,0:T(8,128)}), f32[32,4,64,128]{3,2,1,0:T(8,128)}) %all-gather.23.cloned.1.call-update) | async-done | bytes 4194320 | tf_op jit(solution)/shard_map/all_gather | solution.py:10
  625.9 4.8 reverse_bitcast_fusion
  630.7 32.0 %while.31 = (s32[]{:T(128)}, f32[1,4,64,128]{3,2,1,0:T(8,128)S(1)}, s32[]{:T(128)}, f32[32,1,4]{2,1,0:T(1,128)S(1)}, f32[32,1,4,64,128]{4,3,2,1,0:T(8,128)}, /*index=5*/s32[]{:T(128)}, s32[]{:T(128)}) while((s32[]{:T(128)}, f32[1,4,64,128]{3,2,1,0:T(8,128)S(1)}, s32[]{:T(128)}, f32[32,1,4]{2,1,0:T(1,128)S(1)}, ...), condition=%wide.region_8.9_spmd.clone, body=%wide.region_7.8_spmd.clone.sunk | while | flops 131076 | bytes 393369 | solution.py:22
  631.8 1.0 fusion.113
  632.8 1.0 fusion.113
  633.8 1.0 fusion.113
  (242 shorter events, 110.9 us)
Async XLA Ops:
  7.2 132.1 %copy-start = (bf16[128,4096]{1,0:T(8,128)(2,1)S(1)}, bf16[128,4096]{1,0:T(8,128)(2,1)}, u32[]{:S(2)}) copy-start(bf16[128,4096]{1,0:T(8,128)(2,1)} %param.20) | copy-start | bytes 3145732
  7.2 70.7 %all-gather.13.cloned.1.call-start = ((), (), s32[]{:S(2)}) async-start(), calls=%async_computation | async-start | bytes 2162688 | tf_op jit(solution)/shard_map/all_gather | solution.py:80
  9.1 130.2 %all-gather.15.cloned.1.call-start = ((), (), s32[]{:S(2)}) async-start(), calls=%async_computation.1 | async-start | bytes 2162688 | tf_op jit(solution)/shard_map/all_gather | solution.py:81
  10.9 276.1 %all-reduce.2.cloned.1.call-start = ((), (), s32[]{:S(2)}) async-start(), calls=%async_computation.2 | async-start | bytes 4194304 | tf_op jit(solution)/shard_map/psum | solution.py:108
  83.6 3.3 copy-start.1
  90.6 58.0 %copy-start.11 = (bf16[128,4,256]{2,1,0:T(4,128)(2,1)S(1)}, bf16[128,4,256]{2,1,0:T(4,128)(2,1)}, u32[]{:S(2)}) copy-start(bf16[128,4,256]{2,1,0:T(4,128)(2,1)} %param.23) | copy-start | bytes 786436
  90.6 58.9 %copy-start.14 = (bf16[128,4]{0,1:T(4,128)(2,1)S(1)}, bf16[128,4]{0,1:T(4,128)(2,1)}, u32[]{:S(2)}) copy-start(bf16[128,4]{0,1:T(4,128)(2,1)} %param.24) | copy-start | bytes 3076
  90.6 101.8 %copy-start.17 = (f32[4]{0:T(128)S(1)}, f32[4]{0:T(128)}, u32[]{:S(2)}) copy-start(f32[4]{0:T(128)} %param.26) | copy-start | bytes 52
  148.0 210.9 %copy-start.16 = (f32[4096]{0:T(1024)S(1)}, f32[4096]{0:T(1024)}, u32[]{:S(2)}) copy-start(f32[4096]{0:T(1024)} %param.21) | copy-start | bytes 49156
  148.0 210.9 %all-gather.17.cloned.1.call-start = ((), (), s32[]{:S(2)}) async-start(), calls=%async_computation.3 | async-start | bytes 2162688 | tf_op jit(solution)/shard_map/all_gather | solution.py:127
  148.6 271.5 %all-gather.19.cloned.1.call-start = ((), (), s32[]{:S(2)}) async-start(), calls=%async_computation.4 | async-start | bytes 2162688 | tf_op jit(solution)/shard_map/all_gather | solution.py:132
  149.4 339.7 %all-gather.21.cloned.1.call-start = ((), (), s32[]{:S(2)}) async-start(), calls=%async_computation.5 | async-start | bytes 4325376 | tf_op jit(solution)/shard_map/all_gather | solution.py:10
  290.2 73.0 %copy-start.18 = (f32[4]{0:T(128)S(1)}, f32[4]{0:T(128)}, u32[]{:S(2)}) copy-start(f32[4]{0:T(128)} %param.25) | copy-start | bytes 52
  290.2 73.8 %copy-start.15 = (f32[256]{0:T(256)}, f32[256]{0:T(256)S(1)}, u32[]{:S(2)}) copy-start(f32[256]{0:T(256)S(1)} %add_rsqrt_fusion) | copy-start | bytes 3076
  361.3 2.8 copy-start.9
  363.2 59.3 %copy-start.5 = (bf16[2,128,4,64]{1,3,2,0:T(8,128)(2,1)}, bf16[2,128,4,64]{1,3,2,0:T(8,128)(2,1)S(1)}, u32[]{:S(2)}) copy-start(bf16[2,128,4,64]{1,3,2,0:T(8,128)(2,1)S(1)} %copy.90) | copy-start | bytes 393220
  364.3 60.6 %copy-start.4 = (f32[2,128,1,4]{3,2,1,0:T(1,128)}, f32[2,128,1,4]{3,2,1,0:T(1,128)S(1)}, u32[]{:S(2)}) copy-start(f32[2,128,1,4]{3,2,1,0:T(1,128)S(1)} %fusion.59) | copy-start | bytes 12292
  365.1 60.0 %copy-start.12 = (f32[2,1,4,1]{2,1,3,0:T(1,128)S(1)}, f32[2,1,4,1]{2,1,3,0:T(1,128)}, u32[]{:S(2)}) copy-start(f32[2,1,4,1]{2,1,3,0:T(1,128)} %get-tuple-element.323) | copy-start | bytes 100
  422.5 0.7 copy-start.7
  424.2 137.1 %copy-start.2 = (f32[2,4,64,128]{3,2,1,0:T(8,128)}, f32[2,4,64,128]{3,2,1,0:T(8,128)S(1)}, u32[]{:S(2)}) copy-start(f32[2,4,64,128]{3,2,1,0:T(8,128)S(1)} %convolution_add_fusion.1) | copy-start | bytes 786436
  425.0 201.0 %all-gather.23.cloned.1.call-start = ((), (), s32[]{:S(2)}) async-start(), calls=%async_computation.6 | async-start | bytes 4325376 | tf_op jit(solution)/shard_map/all_gather | solution.py:10
  612.5 50.3 %copy-start.3 = (f32[2,4,64,128]{3,2,1,0:T(8,128)S(1)}, f32[2,4,64,128]{3,2,1,0:T(8,128)}, u32[]{:S(2)}) copy-start(f32[2,4,64,128]{3,2,1,0:T(8,128)} %copy-done.2) | copy-start | bytes 786436
  612.5 50.3 %copy-start.13 = (f32[4]{0:T(128)S(1)}, f32[4]{0:T(128)}, u32[]{:S(2)}) copy-start(f32[4]{0:T(128)} %get-tuple-element.326) | copy-start | bytes 52
  612.5 50.4 %copy-start.8 = (bf16[256,256]{1,0:T(8,128)(2,1)S(1)}, bf16[256,256]{1,0:T(8,128)(2,1)}, u32[]{:S(2)}) copy-start(bf16[256,256]{1,0:T(8,128)(2,1)} %copy-done.7) | copy-start | bytes 393220
  612.5 50.8 %copy-start.6 = (bf16[2,128,4,64]{1,3,2,0:T(8,128)(2,1)S(1)}, bf16[2,128,4,64]{1,3,2,0:T(8,128)(2,1)}, u32[]{:S(2)}) copy-start(bf16[2,128,4,64]{1,3,2,0:T(8,128)(2,1)} %copy-done.5) | copy-start | bytes 393220
  612.5 50.8 %copy-start.10 = (f32[2,128,1,4,64]{1,4,3,0,2:T(8,128)S(1)}, f32[2,128,1,4,64]{1,4,3,0,2:T(8,128)}, u32[]{:S(2)}) copy-start(f32[2,128,1,4,64]{1,4,3,0,2:T(8,128)} %copy.102) | copy-start | bytes 786436
  612.5 50.8 %copy-start.19 = (f32[4]{0:T(128)S(1)}, f32[4]{0:T(128)}, u32[]{:S(2)}) copy-start(f32[4]{0:T(128)} %param.27) | copy-start | bytes 52
Sparse Core Ops, SparseCore 0:
  11.7 66.1 all-gather.12
  81.6 57.6 all-gather.14
  148.1 138.8 all-reduce.1
  290.0 68.8 all-gather.16
  362.4 57.6 all-gather.18
  425.1 63.9 all-gather.20
  561.5 64.4 all-gather.22
where the time goes:
time: 674 us; the launch traced here: 672 us
  waiting for transfers between devices  368 us (55%)
  blocking collectives  129 us (19%)
  other arithmetic  91 us (14%)
  local copies, waits for them, and re-layouts  43.9 us (7%)
  matrix products  24.1 us (4%)
  between operations  14.6 us (2%)
    psum x1, waiting for transfers between devices, body(): lax.psum(head_part.astype(jnp.bfloat16), 'tp').astype(jnp.float32)  94.5 us
    all_gather x2, blocking collectives, prefix(): pieces = jax.tree.map(lambda part: lax.all_gather(part, axis), value)  86.1 us
    select_n x93, other arithmetic, lap(): jnp.where(position < mine, new, old)  81.7 us
    all_gather x1, waiting for transfers between devices, body(): lax.all_gather(x_proj, 'ctx', axis=0, tiled=True)  68.7 us
    all_gather x1, waiting for transfers between devices, body(): key_piece = lax.all_gather(keys_mine, 'ctx', axis=0, tiled=True)  66.9 us
    all_gather x1, waiting for transfers between devices, body(): lax.all_gather(bc_mine, 'ctx', axis=0, tiled=True)  55 us
    all_gather x1, waiting for transfers between devices, body(): value_piece = lax.all_gather(values_mine, 'ctx', axis=0, tiled=True)  48.6 us
    all_gather x1, blocking collectives, body(): lax.all_gather(dt_proj, 'ctx', axis=0, tiled=True)  43 us
  transfers between devices with their start and end apart: 7, of which 7 were waited for; matrix products, arithmetic and copies ran while one was open for 5% of the time, Pallas kernels for 0%

commit v1 on v0

--- a/solution.py
+++ b/solution.py
@@ -77,8 +77,13 @@
     root_dim = math.sqrt(head_dim)
     start_max = jnp.full((kv_local, per_kv, tok_dev), -1e30, jnp.float32)
     run_max = start_max
-    key_piece = lax.all_gather(keys_mine, "ctx", axis=0, tiled=True)
-    value_piece = lax.all_gather(values_mine, "ctx", axis=0, tiled=True)
+    key_piece, value_piece = jnp.split(
+        lax.all_gather(
+            jnp.concatenate([keys_mine, values_mine], axis=1), "ctx", axis=0, tiled=True
+        ),
+        [keys_mine.shape[1]],
+        axis=1,
+    )
     count = key_piece.shape[0]
     key_pos = block_positions(jnp.arange(count, dtype=jnp.int32), tok_dev, n_ctx)
     scores = (

time: 674 us -> 633 us (0.939)
  waiting for transfers between devices: 368 us -> 328 us
    all_gather x2 -> x1, waiting for transfers between devices: 116 us -> 74.8 us  [body(): lax.all_gather(jnp.concatenate([keys_mine, values_mine], axis=1), 'ctx',...]
  transfers between devices with their start and end apart: 7 -> 6, of which waited for: 7 -> 6; matrix products, arithmetic and copies ran while one was open for 5% -> 3% of each run, Pallas kernels for 0% -> 0%
where the time goes in v1:
time: 633 us; the launch traced here: 631 us
  waiting for transfers between devices  328 us (52%)
  blocking collectives  129 us (20%)
  other arithmetic  91.6 us (14%)
  local copies, waits for them, and re-layouts  41.6 us (7%)
  matrix products  24.1 us (4%)
  between operations  14.6 us (2%)
    psum x1, waiting for transfers between devices, body(): lax.psum(head_part.astype(jnp.bfloat16), 'tp').astype(jnp.float32)  95.4 us
    all_gather x2, blocking collectives, prefix(): pieces = jax.tree.map(lambda part: lax.all_gather(part, axis), value)  85.6 us
    select_n x93, other arithmetic, lap(): jnp.where(position < mine, new, old)  81.5 us
    all_gather x1, waiting for transfers between devices, body(): lax.all_gather(jnp.concatenate([keys_mine, values_mine], axis=1), 'ctx',...  74.8 us
    all_gather x1, waiting for transfers between devices, body(): lax.all_gather(x_proj, 'ctx', axis=0, tiled=True)  68.8 us
    all_gather x1, waiting for transfers between devices, body(): lax.all_gather(bc_mine, 'ctx', axis=0, tiled=True)  55 us
    all_gather x1, blocking collectives, body(): lax.all_gather(dt_proj, 'ctx', axis=0, tiled=True)  43.3 us
    all_gather x2, waiting for transfers between devices, prefix(): pieces = jax.tree.map(lambda part: lax.all_gather(part, axis), value)  33.5 us
  transfers between devices with their start and end apart: 6, of which 6 were waited for; matrix products, arithmetic and copies ran while one was open for 3% of the time, Pallas kernels for 0%

profile of v1, /device:TPU:1, one launch (start us, length us, event | category | flops | bytes accessed | tf_op | source)
XLA Modules:
  0.0 630.5 jit_solution(15013991735184943240)
XLA Ops:
  7.2 1.4 constant_dynamic-slice_fusion.3
  9.5 74.8 %all-gather.12.cloned.1.call-done = bf16[8192,2,128]{2,0,1:T(8,128)(2,1)} async-done(((bf16[256,2,128]{2,0,1:T(8,128)(2,1)}), bf16[8192,2,128]{2,0,1:T(8,128)(2,1)}) %all-gather.12.cloned.1.call-update) | async-done | bytes 4194320 | tf_op jit(solution)/shard_map/all_gather | solution.py:81
  84.3 5.7 fusion.4
  90.0 3.2 copy-done.1
  93.3 3.7 fusion.5
  97.0 8.6 %convolution_convert_fusion = bf16[256,4096]{1,0:T(8,128)(2,1)} fusion(bf16[128,4096]{1,0:T(8,128)(2,1)S(1)} %copy-done, bf16[8192,2,128]{2,0,1:T(8,128)(2,1)} %all-gather.12.cloned.1.call-done, f32[1,1,256,8192]{2,3,1,0:T(8,128)} %copy-done.1, f32[256]{0:T(256)S(1)} %broadcast_maximum_fusion, s32[256]{0:T(256)S(1)} %fusion.80, s32[8192]{0:T(1024)S(1)} %fusion.75, ...), kind=kOutput, calls=%fused_computation.18 | convolution fusion | flops 814809088 | bytes 13667328 | tf_op jit(solution)/shard_map/dot_general | solution.py:111
  107.4 43.3 %all_gather.33 = bf16[4096,4]{0,1:T(4,128)(2,1)S(1)} all-gather(bf16[128,4]{0,1:T(4,128)(2,1)S(1)} %copy-done.14), channel_id=1, replica_groups=mesh['ctx'=32,'tp'=16] {'ctx'}, dimensions={0}, use_global_device_ids=true | all-gather | bytes 33792 | tf_op jit(solution)/shard_map/all_gather | solution.py:142
  150.7 95.4 %all-reduce.2.cloned.1.call-done = bf16[256,4096]{1,0:T(8,128)(2,1)} async-done(((bf16[256,4096]{1,0:T(8,128)(2,1)}), bf16[256,4096]{1,0:T(8,128)(2,1)}) %all-reduce.2.cloned.1.call-update) | async-done | bytes 2097168 | tf_op jit(solution)/shard_map/psum | solution.py:113
  246.1 3.2 fusion.7
  249.3 68.8 %all-gather.14.cloned.1.call-done = bf16[4096,256]{1,0:T(8,128)(2,1)} async-done(((bf16[128,256]{1,0:T(8,128)(2,1)}), bf16[4096,256]{1,0:T(8,128)(2,1)}) %all-gather.14.cloned.1.call-update) | async-done | bytes 2097168 | tf_op jit(solution)/shard_map/all_gather | solution.py:132
  318.2 2.4 convolution_convert_fusion.1
  321.4 1.1 copy.90
  324.4 55.0 %all-gather.16.cloned.1.call-done = bf16[4096,1,256]{2,0,1:T(8,128)(2,1)} async-done(((bf16[128,1,256]{2,0,1:T(8,128)(2,1)}), bf16[4096,1,256]{2,0,1:T(8,128)(2,1)}) %all-gather.16.cloned.1.call-update) | async-done | bytes 2097168 | tf_op jit(solution)/shard_map/all_gather | solution.py:137
  379.4 2.4 fusion.22
  382.4 1.1 convolution_add_fusion.1
  384.9 43.3 %all-gather.1 = f32[32,1,4,1]{2,3,1,0:T(1,128)} all-gather(f32[1,1,4,1]{2,3,1,0:T(1,128)S(1)} %get-tuple-element.328), channel_id=3, replica_groups=mesh['ctx'=32,'tp'=16] {'ctx'}, dimensions={0}, use_global_device_ids=true | all-gather | bytes 528 | tf_op jit(solution)/shard_map/all_gather | solution.py:10
  428.3 20.1 %all-gather.18.cloned.1.call-done = f32[32,4,64,128]{3,2,1,0:T(8,128)} async-done(((f32[1,4,64,128]{3,2,1,0:T(8,128)}), f32[32,4,64,128]{3,2,1,0:T(8,128)}) %all-gather.18.cloned.1.call-update) | async-done | bytes 4194320 | tf_op jit(solution)/shard_map/all_gather | solution.py:10
  448.4 70.5 %while.30 = (s32[]{:T(128)}, f32[1,4]{1,0:T(1,128)S(1)}, f32[1,4,64,128]{3,2,1,0:T(8,128)S(1)}, s32[]{:T(128)}, f32[32,1,4]{2,1,0:T(1,128)}, /*index=5*/f32[32,1,4,64,128]{4,3,2,1,0:T(8,128)}, s32[]{:T(128)}, s32[]{:T(128)}) while((s32[]{:T(128)}, f32[1,4]{1,0:T(1,128)S(1)}, f32[1,4,64,128]{3,2,1,0:T(8,128)S(1)}, s32[]{:T(128)}, ...), condition=%wide.region_6.7_spmd.clone, body=%wide.region_5.6_spmd.clone.sunk | while | flops 131088 | bytes 393431 | solution.py:22
  518.9 1.4 add_select_fusion
  520.4 2.0 reshape.405
  523.3 2.0 copy.102
  525.9 1.0 fusion.57
  527.0 1.3 fusion.42
  528.9 42.3 %all-gather.5 = f32[32,1,4]{2,1,0:T(1,128)S(1)} all-gather(f32[1,1,4]{2,1,0:T(1,128)S(1)} %fusion.83), channel_id=5, replica_groups=mesh['ctx'=32,'tp'=16] {'ctx'}, dimensions={0}, use_global_device_ids=true | all-gather | bytes 528 | tf_op jit(solution)/shard_map/all_gather | solution.py:10
  571.5 13.4 %all-gather.20.cloned.1.call-done = f32[32,4,64,128]{3,2,1,0:T(8,128)} async-done(((f32[1,4,64,128]{3,2,1,0:T(8,128)}), f32[32,4,64,128]{3,2,1,0:T(8,128)}) %all-gather.20.cloned.1.call-update) | async-done | bytes 4194320 | tf_op jit(solution)/shard_map/all_gather | solution.py:10
  584.9 4.8 reverse_bitcast_fusion
  589.7 32.0 %while.31 = (s32[]{:T(128)}, f32[1,4,64,128]{3,2,1,0:T(8,128)S(1)}, s32[]{:T(128)}, f32[32,1,4]{2,1,0:T(1,128)S(1)}, f32[32,1,4,64,128]{4,3,2,1,0:T(8,128)}, /*index=5*/s32[]{:T(128)}, s32[]{:T(128)}) while((s32[]{:T(128)}, f32[1,4,64,128]{3,2,1,0:T(8,128)S(1)}, s32[]{:T(128)}, f32[32,1,4]{2,1,0:T(1,128)S(1)}, ...), condition=%wide.region_8.9_spmd.clone, body=%wide.region_7.8_spmd.clone.sunk | while | flops 131076 | bytes 393369 | solution.py:22
  590.8 1.0 fusion.105
  591.8 1.0 fusion.105
  593.9 1.0 fusion.105
  594.9 1.0 fusion.105
  595.9 1.0 fusion.105
  (239 shorter events, 108.1 us)
Async XLA Ops:
  7.2 89.8 %copy-start = (bf16[128,4096]{1,0:T(8,128)(2,1)S(1)}, bf16[128,4096]{1,0:T(8,128)(2,1)}, u32[]{:S(2)}) copy-start(bf16[128,4096]{1,0:T(8,128)(2,1)} %param.20) | copy-start | bytes 3145732
  7.2 77.1 %all-gather.12.cloned.1.call-start = ((), (), s32[]{:S(2)}) async-start(), calls=%async_computation | async-start | bytes 4325376 | tf_op jit(solution)/shard_map/all_gather | solution.py:81
  9.4 236.8 %all-reduce.2.cloned.1.call-start = ((), (), s32[]{:S(2)}) async-start(), calls=%async_computation.1 | async-start | bytes 4194304 | tf_op jit(solution)/shard_map/psum | solution.py:113
  90.0 3.3 copy-start.1
  97.0 9.5 %copy-start.11 = (bf16[128,4,256]{2,1,0:T(4,128)(2,1)S(1)}, bf16[128,4,256]{2,1,0:T(4,128)(2,1)}, u32[]{:S(2)}) copy-start(bf16[128,4,256]{2,1,0:T(4,128)(2,1)} %param.23) | copy-start | bytes 786436
  97.0 10.4 %copy-start.14 = (bf16[128,4]{0,1:T(4,128)(2,1)S(1)}, bf16[128,4]{0,1:T(4,128)(2,1)}, u32[]{:S(2)}) copy-start(bf16[128,4]{0,1:T(4,128)(2,1)} %param.24) | copy-start | bytes 3076
  97.0 53.7 %copy-start.17 = (f32[4]{0:T(128)S(1)}, f32[4]{0:T(128)}, u32[]{:S(2)}) copy-start(f32[4]{0:T(128)} %param.26) | copy-start | bytes 52
  105.7 212.5 %copy-start.16 = (f32[4096]{0:T(1024)S(1)}, f32[4096]{0:T(1024)}, u32[]{:S(2)}) copy-start(f32[4096]{0:T(1024)} %param.21) | copy-start | bytes 49156
  105.7 212.5 %all-gather.14.cloned.1.call-start = ((), (), s32[]{:S(2)}) async-start(), calls=%async_computation.2 | async-start | bytes 2162688 | tf_op jit(solution)/shard_map/all_gather | solution.py:132
  106.4 272.9 %all-gather.16.cloned.1.call-start = ((), (), s32[]{:S(2)}) async-start(), calls=%async_computation.3 | async-start | bytes 2162688 | tf_op jit(solution)/shard_map/all_gather | solution.py:137
  107.3 341.0 %all-gather.18.cloned.1.call-start = ((), (), s32[]{:S(2)}) async-start(), calls=%async_computation.4 | async-start | bytes 4325376 | tf_op jit(solution)/shard_map/all_gather | solution.py:10
  249.3 73.2 %copy-start.18 = (f32[4]{0:T(128)S(1)}, f32[4]{0:T(128)}, u32[]{:S(2)}) copy-start(f32[4]{0:T(128)} %param.25) | copy-start | bytes 52
  249.3 73.9 %copy-start.15 = (f32[256]{0:T(256)}, f32[256]{0:T(256)S(1)}, u32[]{:S(2)}) copy-start(f32[256]{0:T(256)S(1)} %add_rsqrt_fusion) | copy-start | bytes 3076
  320.5 2.8 copy-start.9
  322.5 59.3 %copy-start.5 = (bf16[2,128,4,64]{1,3,2,0:T(8,128)(2,1)}, bf16[2,128,4,64]{1,3,2,0:T(8,128)(2,1)S(1)}, u32[]{:S(2)}) copy-start(bf16[2,128,4,64]{1,3,2,0:T(8,128)(2,1)S(1)} %copy.90) | copy-start | bytes 393220
  323.6 60.7 %copy-start.4 = (f32[2,128,1,4]{3,2,1,0:T(1,128)}, f32[2,128,1,4]{3,2,1,0:T(1,128)S(1)}, u32[]{:S(2)}) copy-start(f32[2,128,1,4]{3,2,1,0:T(1,128)S(1)} %fusion.51) | copy-start | bytes 12292
  324.4 60.0 %copy-start.12 = (f32[2,1,4,1]{2,1,3,0:T(1,128)S(1)}, f32[2,1,4,1]{2,1,3,0:T(1,128)}, u32[]{:S(2)}) copy-start(f32[2,1,4,1]{2,1,3,0:T(1,128)} %get-tuple-element.323) | copy-start | bytes 100
  381.8 0.7 copy-start.7
  383.5 136.8 %copy-start.2 = (f32[2,4,64,128]{3,2,1,0:T(8,128)}, f32[2,4,64,128]{3,2,1,0:T(8,128)S(1)}, u32[]{:S(2)}) copy-start(f32[2,4,64,128]{3,2,1,0:T(8,128)S(1)} %convolution_add_fusion.1) | copy-start | bytes 786436
  384.2 200.7 %all-gather.20.cloned.1.call-start = ((), (), s32[]{:S(2)}) async-start(), calls=%async_computation.5 | async-start | bytes 4325376 | tf_op jit(solution)/shard_map/all_gather | solution.py:10
  571.5 50.2 %copy-start.3 = (f32[2,4,64,128]{3,2,1,0:T(8,128)S(1)}, f32[2,4,64,128]{3,2,1,0:T(8,128)}, u32[]{:S(2)}) copy-start(f32[2,4,64,128]{3,2,1,0:T(8,128)} %copy-done.2) | copy-start | bytes 786436
  571.5 50.2 %copy-start.13 = (f32[4]{0:T(128)S(1)}, f32[4]{0:T(128)}, u32[]{:S(2)}) copy-start(f32[4]{0:T(128)} %get-tuple-element.326) | copy-start | bytes 52
  571.5 50.3 %copy-start.8 = (bf16[256,256]{1,0:T(8,128)(2,1)S(1)}, bf16[256,256]{1,0:T(8,128)(2,1)}, u32[]{:S(2)}) copy-start(bf16[256,256]{1,0:T(8,128)(2,1)} %copy-done.7) | copy-start | bytes 393220
  571.5 50.7 %copy-start.6 = (bf16[2,128,4,64]{1,3,2,0:T(8,128)(2,1)S(1)}, bf16[2,128,4,64]{1,3,2,0:T(8,128)(2,1)}, u32[]{:S(2)}) copy-start(bf16[2,128,4,64]{1,3,2,0:T(8,128)(2,1)} %copy-done.5) | copy-start | bytes 393220
  571.5 50.7 %copy-start.10 = (f32[2,128,1,4,64]{1,4,3,0,2:T(8,128)S(1)}, f32[2,128,1,4,64]{1,4,3,0,2:T(8,128)}, u32[]{:S(2)}) copy-start(f32[2,128,1,4,64]{1,4,3,0,2:T(8,128)} %copy.102) | copy-start | bytes 786436
  571.5 50.7 %copy-start.19 = (f32[4]{0:T(128)S(1)}, f32[4]{0:T(128)}, u32[]{:S(2)}) copy-start(f32[4]{0:T(128)} %param.27) | copy-start | bytes 52
Sparse Core Ops, SparseCore 0:
  11.8 72.4 all-gather.11
  105.8 140.2 all-reduce.1
  249.3 68.8 all-gather.13
  321.7 57.6 all-gather.15
  384.4 63.9 all-gather.17
  520.4 64.4 all-gather.19
